TPU v7x, 32 devices: a whole 2x2x4 slice. The times are simulated.
32 devices in a mesh: grp: 2 (over y), slab: 4 (over z), head: 2 (over x), seq: 2 (over core).
Axes of the slice: x: 2, y: 2, z: 4, core: 2. Of those that a mesh axis runs over, the one named last changes fastest.
Arguments:
- queries: bfloat16 [1024, 5120], P(('grp', 'seq'), 'head'), parts along dimension 0, may hold values from -140 to 140
- query_gain: float32 [5120], P('head'), may hold values from 1.5 to 3
- cache_keys: bfloat16 [4096, 5120], P(('grp', 'slab'), 'head'), parts along dimension 0, may hold values from -120 to 120
- cache_values: bfloat16 [4096, 5120], P(('grp', 'slab'), 'head'), parts along dimension 0, may hold values from -6 to 6
- finished_keys: bfloat16 [1024, 5120], P(('grp', 'slab', 'seq'), 'head'), parts along dimension 0, may hold values from -6 to 6
- finished_values: bfloat16 [1024, 5120], P(('grp', 'slab', 'seq'), 'head'), parts along dimension 0, may hold values from -6 to 6
- new_keys: bfloat16 [1024, 5120], P(('grp', 'slab', 'seq'), 'head'), parts along dimension 0, may hold values from -6 to 6
- new_values: bfloat16 [1024, 5120], P(('grp', 'slab', 'seq'), 'head'), parts along dimension 0, may hold values from -6 to 6
- out_weight: bfloat16 [5120, 5120], P('head', 'slab'), may hold values from -0.25 to 0.25
- time_weight: float32 [256, 5120], P(None, ('slab', 'head')), may hold values from -0.375 to 0.375
- owner: int32 [2], P('grp'), parts along dimension 0, may hold values from 0 to 3
- step: int32 [2], P('grp'), parts along dimension 0, may hold values from 0 to 999
Outputs:
- branch: bfloat16 [1024, 5120], P(('grp', 'seq'), ('slab', 'head')), parts along dimension 0
There are 2 independent parts, one for each index of `grp`. A program takes and returns all parts, laid end to end along the dimension named above; an argument that names none is the same for every part. Nothing has to cross between parts.
All inputs are finite; a program needn't handle non-finite values.
Results may differ from a plain program's by a relative error of at most 0.012.
Values may be sent and summed in bfloat16 or wider, within the bound.
No kernel may reach another device: no remote copies, remote signals or barrier semaphores. Data moves between devices by JAX's collectives and lax.ppermute only.
A program may use at most 64 MiB of HBM per device.

v0:
```python
from functools import reduce
import jax
import jax.numpy as jnp
from jax import lax
from jax.sharding import PartitionSpec as P

HEADS = 40
HD = 128
EPSILON = 1e-06


def local(
    queries,
    query_gain,
    cache_keys,
    cache_values,
    finished_keys,
    finished_values,
    new_keys,
    new_values,
    out_weight,
    time_weight,
    owner,
    step,
):
    row_count = queries.shape[0]
    head_count = queries.shape[1] // HD
    query_float = queries.astype(jnp.float32)
    norm_total = lax.psum(jnp.sum(query_float * query_float, axis=1), "head")
    inverse = lax.rsqrt(norm_total / (HEADS * HD) + EPSILON)
    normed = (
        (query_float * inverse[:, None] * query_gain)
        .astype(jnp.bfloat16)
        .reshape(row_count, head_count, HD)
    )
    is_owner = lax.axis_index("slab") == owner[0]
    whole_keys, whole_values = (
        lax.all_gather(finished_keys, ("slab", "seq"), axis=0, tiled=True),
        lax.all_gather(finished_values, ("slab", "seq"), axis=0, tiled=True),
    )
    fresh_keys, fresh_values = (
        lax.all_gather(new_keys, "seq", axis=0, tiled=True),
        lax.all_gather(new_values, "seq", axis=0, tiled=True),
    )
    key_block = jnp.where(is_owner, whole_keys, cache_keys)
    value_block = jnp.where(is_owner, whole_values, cache_values)
    blocks = [
        (key_block, value_block, jnp.float32(0.0)),
        (fresh_keys, fresh_values, jnp.float32(0.0)),
    ]
    score_scale = 1.0 / HD**0.5
    score_list = []
    for key_block, value_block, penalty in blocks:
        key_heads = key_block.reshape(key_block.shape[0], head_count, HD)
        each_score = jnp.einsum(
            "rhd,khd->hrk", normed, key_heads, preferred_element_type=jnp.float32
        )
        score_list.append(each_score * score_scale)
    row_top = reduce(jnp.maximum, [jnp.max(each_score, axis=2) for each_score in score_list])
    row_mass = jnp.zeros_like(row_top)
    partial_value = jnp.zeros((head_count, row_count, HD), jnp.float32)
    for each_score, (key_block, value_block, penalty) in zip(score_list, blocks):
        raw_weights = jnp.exp(each_score - row_top[:, :, None])
        row_mass = row_mass + jnp.sum(raw_weights, axis=2)
        value_heads = value_block.reshape(value_block.shape[0], head_count, HD)
        partial_value = partial_value + jnp.einsum(
            "hrk,khd->hrd",
            raw_weights.astype(jnp.bfloat16),
            value_heads,
            preferred_element_type=jnp.float32,
        )
    global_top = lax.pmax(row_top, "slab")
    factor = jnp.exp(row_top - global_top)
    sum_share, mass_share = (
        lax.psum_scatter(
            partial_value * factor[:, :, None], "slab", scatter_dimension=1, tiled=True
        ),
        lax.psum_scatter(row_mass * factor, "slab", scatter_dimension=1, tiled=True),
    )
    row_share = (sum_share / mass_share[:, :, None]).astype(jnp.bfloat16)
    attended = lax.all_gather(row_share, "slab", axis=1, tiled=True)
    weight_heads = out_weight.reshape(head_count, HD, out_weight.shape[1])
    projected = jnp.einsum(
        "hrd,hdc->rc", attended, weight_heads, preferred_element_type=jnp.float32
    )
    summed = lax.psum_scatter(projected, "head", scatter_dimension=1, tiled=True)
    half = time_weight.shape[0] // 2
    frequency = jnp.exp(-jnp.log(10000.0) * jnp.arange(half, dtype=jnp.float32) / half)
    phases = step[0].astype(jnp.float32) * frequency
    embedding = jnp.concatenate([jnp.cos(phases), jnp.sin(phases)])
    time_gate = 1.0 + jnp.dot(embedding, time_weight, precision=lax.Precision.HIGHEST)
    return (time_gate * summed).astype(jnp.bfloat16)


def solution(mesh):
    in_specs = (
        P(("grp", "seq"), "head"),
        P("head"),
        P(("grp", "slab"), "head"),
        P(("grp", "slab"), "head"),
        P(("grp", "slab", "seq"), "head"),
        P(("grp", "slab", "seq"), "head"),
        P(("grp", "slab", "seq"), "head"),
        P(("grp", "slab", "seq"), "head"),
        P("head", "slab"),
        P(None, ("slab", "head")),
        P("grp"),
        P("grp"),
    )
    out_specs = P(("grp", "seq"), ("slab", "head"))
    return jax.shard_map(local, mesh=mesh, in_specs=in_specs, out_specs=out_specs, check_vma=False)
```

profile of v0, /device:TPU:0, one launch (start us, length us, event | category | flops | bytes accessed | tf_op | source)
XLA Modules:
  0.0 240.0 jit_solution(8406601955525841598)
XLA Ops:
  6.5 0.7 all-gather.4.cloned.1.call-update
  7.3 0.7 all-gather.6.cloned.1.call-update
  8.1 4.5 %copy.36 = bf16[512,2560]{0,1:T(8,128)(2,1)} copy(bf16[512,2560]{1,0:T(8,128)(2,1)} %param.15) | data formatting | bytes 5242880 | tf_op args[3]
  13.3 0.6 copy.27
  13.9 4.5 %copy.29 = bf16[512,2560]{0,1:T(8,128)(2,1)} copy(bf16[512,2560]{1,0:T(8,128)(2,1)} %param.14) | data formatting | bytes 5242880 | tf_op args[2]
  18.4 2.7 %all_gather.16 = bf16[128,2560]{1,0:T(8,128)(2,1)S(1)} all-gather(bf16[64,2560]{1,0:T(8,128)(2,1)S(1)} %copy-done.4), channel_id=1, replica_groups=mesh['grp'=2,'slab'=4,'head'=2,'seq'=2] {'seq'}, dimensions={0}, use_global_device_ids=true | all-gather | bytes 983040 | tf_op jit(solution)/shard_map/all_gather | solution.py:42
  21.1 1.1 copy.32
  22.2 2.3 all_gather.18
  24.4 1.1 copy.38
  25.9 5.5 %psum.7 = f32[256]{0:T(256)S(1)} all-reduce(f32[256]{0:T(256)S(1)} %fusion.6), channel_id=1, replica_groups=mesh['grp'=2,'slab'=4,'head'=2,'seq'=2] {'head'}, use_global_device_ids=true, to_apply=%region_1.0 | all-reduce | flops 256 | bytes 2048 | tf_op jit(solution)/shard_map/psum | solution.py:29
  31.9 1.2 copy-done.1
  33.0 1.7 multiply_reduce_fusion.1
  34.7 10.7 %all-gather.4.cloned.1.call-done = bf16[512,2560]{1,0:T(8,128)(2,1)} async-done(((bf16[64,2560]{1,0:T(8,128)(2,1)}), bf16[512,2560]{1,0:T(8,128)(2,1)}) %all-gather.4.cloned.1.call-update) | async-done | bytes 2621456 | tf_op jit(solution)/shard_map/all_gather | solution.py:38
  45.4 4.4 %copy.28 = bf16[512,2560]{0,1:T(8,128)(2,1)} copy(bf16[512,2560]{1,0:T(8,128)(2,1)} %all-gather.4.cloned.1.call-done) | data formatting | bytes 5242880 | tf_op jit(solution)/shard_map/all_gather | solution.py:38
  49.8 2.1 broadcast_select_fusion.1
  52.0 5.7 %multiply_reduce_fusion = (f32[20,256]{1,0:T(8,128)S(1)}, f32[20,256,512]{2,1,0:T(8,128)}) fusion(bf16[256,20,128]{0,2,1:T(8,128)(2,1)S(1)} %bitcast.25, bf16[512,20,128]{0,2,1:T(8,128)(2,1)S(1)} %bitcast.27), kind=kOutput, calls=%fused_computation.1 | convolution fusion | flops 676326400 | bytes 14438400 | tf_op jit(solution)/shard_map/rhd,khd->hrk/dot_general | solution.py:55
  57.6 18.7 %pmax.7 = f32[20,256]{1,0:T(8,128)S(1)} all-reduce(f32[20,256]{1,0:T(8,128)S(1)} %max.9), channel_id=1, replica_groups=mesh['grp'=2,'slab'=4,'head'=2,'seq'=2] {'slab'}, use_global_device_ids=true, to_apply=%region_4.5 | all-reduce | flops 5120 | bytes 40960 | tf_op jit(solution)/shard_map/pmax | solution.py:72
  76.4 5.9 %fusion = f32[20,256]{1,0:T(8,128)S(1)} fusion(f32[20,256,512]{2,1,0:T(8,128)} %get-tuple-element.8, f32[20,256]{1,0:T(8,128)S(1)} %max.9), kind=kLoop, calls=%fused_computation.2 | loop fusion | flops 7859200 | bytes 10526720 | tf_op jit(solution)/shard_map/reduce_sum | solution.py:64
  82.3 4.4 %copy.35 = bf16[512,2560]{0,1:T(8,128)(2,1)} copy(bf16[512,2560]{1,0:T(8,128)(2,1)} %all-gather.6.cloned.1.call-done) | data formatting | bytes 5242880 | tf_op jit(solution)/shard_map/all_gather | solution.py:39
  86.7 2.0 broadcast_select_fusion
  88.7 7.7 %fusion.2 = f32[20,256,128]{2,1,0:T(8,128)} fusion(bf16[512,20,128]{0,2,1:T(8,128)(2,1)S(1)} %bitcast.26, f32[20,256,512]{2,1,0:T(8,128)} %get-tuple-element.8, f32[20,256]{1,0:T(8,128)S(1)} %max.9), kind=kOutput, calls=%fused_computation.4 | convolution fusion | flops 678952960 | bytes 15749120 | tf_op jit(solution)/shard_map/hrk,khd->hrd/dot_general | solution.py:66
  96.4 0.5 fusion.9
  96.9 0.8 copy.48
  97.7 4.1 %add_multiply_fusion = f32[20,256,128]{2,1,0:T(8,128)} fusion(f32[20,256,128]{2,1,0:T(8,128)} %fusion.2, bf16[128,20,128]{0,2,1:T(8,128)(2,1)} %bitcast.28, f32[20,256,128]{1,2,0:T(8,128)S(1)} %get-tuple-element.10, f32[20,256]{1,0:T(8,128)S(1)} %get-tuple-element.6, f32[20,256]{1,0:T(8,128)S(1)} %max.9), kind=kOutput, calls=%fused_computation.13 | convolution fusion | flops 171048960 | bytes 8560640 | tf_op jit(solution)/shard_map/hrk,khd->hrd/dot_general | solution.py:66
  101.9 13.7 %reduce-scatter.10.cloned.1.call-done = f32[64,20]{1,0:T(8,128)} async-done(((f32[256,20]{1,0:T(8,128)}), f32[64,20]{1,0:T(8,128)}) %reduce-scatter.10.cloned.1.call-update) | async-done | bytes 5136
  115.6 0.8 copy.49
  116.4 51.8 %reduce-scatter.6.cloned.1.call-done = f32[20,64,128]{2,1,0:T(8,128)} async-done(((f32[20,256,128]{2,1,0:T(8,128)}), f32[20,64,128]{2,1,0:T(8,128)}) %reduce-scatter.6.cloned.1.call-update) | async-done | bytes 655376 | tf_op jit(solution)/shard_map/reduce_scatter | solution.py:75
  168.2 2.1 divide_convert_fusion
  170.4 32.2 %all-gather.8.cloned.1.call-done = bf16[20,256,128]{2,1,0:T(8,128)(2,1)} async-done(((bf16[20,64,128]{2,1,0:T(8,128)(2,1)}), bf16[20,256,128]{2,1,0:T(8,128)(2,1)}) %all-gather.8.cloned.1.call-update) | async-done | bytes 1310736 | tf_op jit(solution)/shard_map/all_gather | solution.py:81
  202.5 6.2 %convolution_bitcast_fusion = f32[256,1280]{1,0:T(8,128)} fusion(bf16[20,256,128]{2,1,0:T(8,128)(2,1)} %all-gather.8.cloned.1.call-done, bf16[20,128,1280]{2,1,0:T(8,128)(2,1)} %bitcast.33), kind=kOutput, calls=%fused_computation.9 | convolution fusion | flops 1677721600 | bytes 9175040 | tf_op jit(solution)/shard_map/hrd,hdc->rc/dot_general | solution.py:83
  209.9 21.4 %reduce-scatter.8.cloned.1.call-done = f32[256,640]{1,0:T(8,128)} async-done(((f32[256,1280]{1,0:T(8,128)}), f32[256,640]{1,0:T(8,128)}) %reduce-scatter.8.cloned.1.call-update) | async-done | bytes 655376 | tf_op jit(solution)/shard_map/reduce_scatter | solution.py:86
  231.3 1.9 multiply_convert_fusion
  (33 shorter events, 1.6 us)
Async XLA Ops:
  6.5 202.9 %copy-start = (f32[256,640]{1,0:T(8,128)S(1)}, f32[256,640]{1,0:T(8,128)}, u32[]{:S(2)}) copy-start(f32[256,640]{1,0:T(8,128)} %param.21) | copy-start | bytes 1966084
  6.5 38.9 %all-gather.4.cloned.1.call-start = ((), (), s32[]{:S(2)}) async-start(), calls=%async_computation.3 | async-start | bytes 2949120 | tf_op jit(solution)/shard_map/all_gather | solution.py:38
  7.3 75.0 %all-gather.6.cloned.1.call-start = ((), (), s32[]{:S(2)}) async-start(), calls=%async_computation.4 | async-start | bytes 2949120 | tf_op jit(solution)/shard_map/all_gather | solution.py:39
  8.0 107.6 %reduce-scatter.10.cloned.1.call-start = ((), (), s32[]{:S(2)}) async-start(), calls=%async_computation.8 | async-start | bytes 163840
  8.1 5.2 %copy-start.3 = (bf16[256,2560]{1,0:T(8,128)(2,1)S(1)}, bf16[256,2560]{1,0:T(8,128)(2,1)}, u32[]{:S(2)}) copy-start(bf16[256,2560]{1,0:T(8,128)(2,1)} %param.12) | copy-start | bytes 3932164
  13.9 4.5 %copy-start.4 = (bf16[64,2560]{1,0:T(8,128)(2,1)S(1)}, bf16[64,2560]{1,0:T(8,128)(2,1)}, u32[]{:S(2)}) copy-start(bf16[64,2560]{1,0:T(8,128)(2,1)} %param.18) | copy-start | bytes 983044
  13.9 8.3 %copy-start.5 = (bf16[64,2560]{1,0:T(8,128)(2,1)S(1)}, bf16[64,2560]{1,0:T(8,128)(2,1)}, u32[]{:S(2)}) copy-start(bf16[64,2560]{1,0:T(8,128)(2,1)} %param.19) | copy-start | bytes 983044
  21.1 10.4 %copy-start.6 = (f32[2560]{0:T(1024)S(1)}, f32[2560]{0:T(1024)}, u32[]{:S(2)}) copy-start(f32[2560]{0:T(1024)} %param.13) | copy-start | bytes 30724
  31.9 1.2 copy-start.1
  49.8 2.1 copy-start.2
  97.7 70.6 %reduce-scatter.6.cloned.1.call-start = ((), (), s32[]{:S(2)}) async-start(), calls=%async_computation.5 | async-start | bytes 3276800 | tf_op jit(solution)/shard_map/reduce_scatter | solution.py:75
  101.8 100.7 %all-gather.8.cloned.1.call-start = ((), (), s32[]{:S(2)}) async-start(), calls=%async_computation.6 | async-start | bytes 1638400 | tf_op jit(solution)/shard_map/all_gather | solution.py:81
  170.3 61.0 %reduce-scatter.8.cloned.1.call-start = ((), (), s32[]{:S(2)}) async-start(), calls=%async_computation.7 | async-start | bytes 1966080 | tf_op jit(solution)/shard_map/reduce_scatter | solution.py:86
Sparse Core Ops, SparseCore 0:
  9.0 36.4 all-gather.3
  47.1 33.8 all-gather.5
  97.8 17.7 reduce-scatter.9
  117.7 50.4 reduce-scatter.5
  170.4 32.0 all-gather.7
  208.9 22.3 reduce-scatter.7
where the time goes:
time: 241 us; the launch traced here: 240 us
  waiting for transfers between devices  131 us (54%)
  blocking collectives  29.2 us (12%)
  matrix products  25.7 us (11%)
  local copies, waits for them, and re-layouts  23.4 us (10%)
  other arithmetic  15.2 us (6%)
  between operations  14.9 us (6%)
    reduce_scatter x1, waiting for transfers between devices, local(): lax.psum_scatter(partial_value * factor[:, :, None], 'slab', scatter_dime...  51.8 us
    all_gather x1, waiting for transfers between devices, local(): attended = lax.all_gather(row_share, 'slab', axis=1, tiled=True)  32.2 us
    reduce_scatter x1, waiting for transfers between devices, local(): lax.psum_scatter(projected, 'head', scatter_dimension=1, tiled=True)  21.4 us
    pmax x1, blocking collectives, local(): global_top = lax.pmax(row_top, 'slab')  18.7 us
    unnamed x7, waiting for transfers between devices  15.2 us
    unnamed x19, local copies, waits for them, and re-layouts  12.4 us
    dot_general x2, matrix products, local(): jnp.einsum('hrk,khd->hrd', raw_weights.astype(jnp.bfloat16), value_heads,...  11.8 us
    all_gather x1, waiting for transfers between devices, local(): lax.all_gather(finished_keys, ('slab', 'seq'), axis=0, tiled=True)  10.7 us
  transfers between devices with their start and end apart: 6, of which 5 were waited for; matrix products, arithmetic and copies ran while one was open for 16% of the time, Pallas kernels for 0%

commit v1 on v0

--- a/solution.py
+++ b/solution.py
@@ -7,6 +7,18 @@
 HEADS = 40
 HD = 128
 EPSILON = 1e-06
+
+
+def collect(x, axis, dim):
+    ways, here, step = (lax.axis_size(axis), lax.axis_index(axis), x.shape[dim])
+    line, have = (x, 1)
+    while have < ways:
+        line = jnp.concatenate(
+            [line, lax.ppermute(line, axis, [(d, (d - have) % ways) for d in range(ways)])],
+            axis=dim,
+        )
+        have = 2 * have
+    return jnp.roll(line, here * step, axis=dim)
 
 
 def local(
@@ -35,7 +47,7 @@
     )
     is_owner = lax.axis_index("slab") == owner[0]
     whole_keys, whole_values = (
-        lax.all_gather(finished_keys, ("slab", "seq"), axis=0, tiled=True),
+        collect(finished_keys, ("slab", "seq"), 0),
         lax.all_gather(finished_values, ("slab", "seq"), axis=0, tiled=True),
     )
     fresh_keys, fresh_values = (

time: 241 us -> 303 us (1.26)
  waiting for transfers between devices: 131 us -> 169 us
  local copies, waits for them, and re-layouts: 23.4 us -> 33.6 us
  blocking collectives: 29.2 us -> 35.9 us
  starting transfers between devices: 0.2 us -> 5.51 us
  other arithmetic: 15.2 us -> 20.4 us
  matrix products: 25.7 us -> 20.7 us
    ppermute x0 -> x3, waiting for transfers between devices: none -> 60.4 us  [collect(): lax.ppermute(line, axis, [(d, (d - have) % ways) for d in range(ways)])]
    unnamed x7 -> x6, waiting for transfers between devices: 15.2 us -> 3.27 us
    all_gather x1 -> x0, waiting for transfers between devices: 10.7 us -> none  [local(): lax.all_gather(finished_keys, ('slab', 'seq'), axis=0, tiled=True)]
    concatenate x0 -> x1, local copies, waits for them, and re-layouts: none -> 9.9 us  [collect(): return jnp.roll(line, here * step, axis=dim)]
    ppermute x0 -> x3, starting transfers between devices: none -> 5.15 us  [collect(): lax.ppermute(line, axis, [(d, (d - have) % ways) for d in range(ways)])]
    all_gather x1 -> x0, local copies, waits for them, and re-layouts: 4.4 us -> none  [local(): lax.all_gather(finished_keys, ('slab', 'seq'), axis=0, tiled=True)]
    all_gather x1, blocking collectives: 2.68 us -> 6.91 us  [local(): lax.all_gather(new_keys, 'seq', axis=0, tiled=True)]
    dot_general x2, matrix products: 11.8 us -> 7.82 us  [local(): jnp.einsum('hrk,khd->hrd', raw_weights.astype(jnp.bfloat16), value_heads,...]
  transfers between devices with their start and end apart: 6 -> 8, of which waited for: 5 -> 6; matrix products, arithmetic and copies ran while one was open for 16% -> 21% of each run, Pallas kernels for 0% -> 0%
where the time goes in v1:
time: 303 us; the launch traced here: 301 us
  waiting for transfers between devices  169 us (56%)
  blocking collectives  35.9 us (12%)
  local copies, waits for them, and re-layouts  33.6 us (11%)
  matrix products  20.7 us (7%)
  other arithmetic  20.4 us (7%)
  between operations  16.5 us (5%)
  starting transfers between devices  5.51 us (2%)
    ppermute x3, waiting for transfers between devices, collect(): lax.ppermute(line, axis, [(d, (d - have) % ways) for d in range(ways)])  60.4 us
    reduce_scatter x1, waiting for transfers between devices, local(): lax.psum_scatter(partial_value * factor[:, :, None], 'slab', scatter_dime...  51.7 us
    all_gather x1, waiting for transfers between devices, local(): attended = lax.all_gather(row_share, 'slab', axis=1, tiled=True)  31.9 us
    reduce_scatter x1, waiting for transfers between devices, local(): lax.psum_scatter(projected, 'head', scatter_dimension=1, tiled=True)  21.4 us
    pmax x1, blocking collectives, local(): global_top = lax.pmax(row_top, 'slab')  20.1 us
    unnamed x22, local copies, waits for them, and re-layouts  14.6 us
    concatenate x1, local copies, waits for them, and re-layouts, collect(): return jnp.roll(line, here * step, axis=dim)  9.9 us
    dot_general x2, matrix products, local(): jnp.einsum('hrk,khd->hrd', raw_weights.astype(jnp.bfloat16), value_heads,...  7.82 us
  transfers between devices with their start and end apart: 8, of which 6 were waited for; matrix products, arithmetic and copies ran while one was open for 21% of the time, Pallas kernels for 0%

profile of v1, /device:TPU:0, one launch (start us, length us, event | category | flops | bytes accessed | tf_op | source)
XLA Modules:
  0.0 301.4 jit_solution(14586637500700692597)
XLA Ops:
  7.4 4.5 %collective-permute-start = (bf16[64,2560]{1,0:T(8,128)(2,1)}, bf16[64,2560]{1,0:T(8,128)(2,1)S(1)}, u32[]{:S(2)}, u32[]{:S(2)}) collective-permute-start(bf16[64,2560]{1,0:T(8,128)(2,1)} %param.16), channel_id=1, source_target_pairs={{0,13},{1,0},{4,1},{5,4},{8,5},{9,8},{12,9},{13,12},{2,15},{3,2},{... | collective-permute-start | bytes 983048 | tf_op jit(solution)/shard_map/ppermute | solution.py:17
  11.9 1.3 copy.36
  13.2 3.6 %collective-permute-done = bf16[64,2560]{1,0:T(8,128)(2,1)S(1)} collective-permute-done((bf16[64,2560]{1,0:T(8,128)(2,1)}, bf16[64,2560]{1,0:T(8,128)(2,1)S(1)}, u32[]{:S(2)}, u32[]{:S(2)}) %collective-permute-start) | collective-permute-done | bytes 327712 | tf_op jit(solution)/shard_map/ppermute | solution.py:17
  17.1 1.2 pad_maximum_fusion.1
  19.0 4.4 %copy.47 = bf16[512,2560]{0,1:T(8,128)(2,1)} copy(bf16[512,2560]{1,0:T(8,128)(2,1)} %param.15) | data formatting | bytes 5242880 | tf_op args[3]
  24.1 1.6 copy.31
  25.7 4.5 %copy.40 = bf16[512,2560]{0,1:T(8,128)(2,1)} copy(bf16[512,2560]{1,0:T(8,128)(2,1)} %param.14) | data formatting | bytes 5242880 | tf_op args[2]
  30.2 6.9 %all_gather.12 = bf16[128,2560]{1,0:T(8,128)(2,1)} all-gather(bf16[64,2560]{1,0:T(8,128)(2,1)} %param.18), channel_id=1, replica_groups=mesh['grp'=2,'slab'=4,'head'=2,'seq'=2] {'seq'}, dimensions={0}, use_global_device_ids=true | all-gather | bytes 983040 | tf_op jit(solution)/shard_map/all_gather | solution.py:54
  37.1 2.2 copy.43
  39.3 4.0 %all_gather.14 = bf16[128,2560]{1,0:T(8,128)(2,1)} all-gather(bf16[64,2560]{1,0:T(8,128)(2,1)} %param.19), channel_id=1, replica_groups=mesh['grp'=2,'slab'=4,'head'=2,'seq'=2] {'seq'}, dimensions={0}, use_global_device_ids=true | all-gather | bytes 983040 | tf_op jit(solution)/shard_map/all_gather | solution.py:55
  43.3 2.2 copy.49
  45.8 4.9 %psum.7 = f32[256]{0:T(256)S(1)} all-reduce(f32[256]{0:T(256)S(1)} %fusion.6), channel_id=1, replica_groups=mesh['grp'=2,'slab'=4,'head'=2,'seq'=2] {'head'}, use_global_device_ids=true, to_apply=%region_1.0 | all-reduce | flops 256 | bytes 2048 | tf_op jit(solution)/shard_map/psum | solution.py:41
  50.8 1.7 pad_maximum_fusion
  53.0 1.2 copy-done.3
  54.8 56.9 %collective-permute-done.2 = bf16[256,2560]{0,1:T(8,128)(2,1)} collective-permute-done((bf16[256,2560]{0,1:T(8,128)(2,1)S(1)}, bf16[256,2560]{0,1:T(8,128)(2,1)}, u32[]{:S(2)}, u32[]{:S(2)}) %collective-permute-start.2) | collective-permute-done | bytes 1310752 | tf_op jit(solution)/shard_map/ppermute | solution.py:17
  111.6 9.9 %concatenate.20 = bf16[1024,2560]{0,1:T(8,128)(2,1)} concatenate(bf16[64,2560]{0,1:T(8,128)(2,1)} %copy-done.1, bf16[64,2560]{0,1:T(8,128)(2,1)} %copy-done.2, bf16[128,2560]{0,1:T(8,128)(2,1)} %collective-permute-done.1, bf16[256,2560]{0,1:T(8,128)(2,1)} %collective-permute-done.2, bf16[64,2560]{0,1:T(8,128)(2,1)} %copy-done.1, bf16[64,2560]{0,1:T(8,128)(2,1)} %copy-done.2, ...), dimensions={0} | concatenate | bytes 10485760 | tf_op jit(solution)/shard_map/jit(_roll_dynamic)/concatenate | solution.py:21
  121.5 4.4 %dynamic-slice_select_fusion = bf16[512,2560]{0,1:T(8,128)(2,1)S(1)} fusion(bf16[512,2560]{0,1:T(8,128)(2,1)} %copy.40, bf16[1024,2560]{0,1:T(8,128)(2,1)} %concatenate.20, s32[]{:T(128)S(6)} %select_n.27, pred[]{:T(512)S(6)} %eq.6), kind=kLoop, calls=%fused_computation.15 | loop fusion | flops 1310720 | bytes 7864325 | tf_op jit(solution)/shard_map/jit(_where)/select_n | solution.py:57
  125.9 5.7 %multiply_reduce_fusion = (f32[20,256]{1,0:T(8,128)S(1)}, f32[20,256,512]{2,1,0:T(8,128)}) fusion(bf16[256,20,128]{0,2,1:T(8,128)(2,1)S(1)} %bitcast.25, bf16[512,20,128]{0,2,1:T(8,128)(2,1)S(1)} %bitcast.27), kind=kOutput, calls=%fused_computation.1 | convolution fusion | flops 676326400 | bytes 14438400 | tf_op jit(solution)/shard_map/rhd,khd->hrk/dot_general | solution.py:67
  131.6 20.1 %pmax.7 = f32[20,256]{1,0:T(8,128)S(1)} all-reduce(f32[20,256]{1,0:T(8,128)S(1)} %max.9), channel_id=1, replica_groups=mesh['grp'=2,'slab'=4,'head'=2,'seq'=2] {'slab'}, use_global_device_ids=true, to_apply=%region_4.5 | all-reduce | flops 5120 | bytes 40960 | tf_op jit(solution)/shard_map/pmax | solution.py:84
  152.2 5.8 %fusion = f32[20,256]{1,0:T(8,128)S(1)} fusion(f32[20,256,512]{2,1,0:T(8,128)} %get-tuple-element.8, f32[20,256]{1,0:T(8,128)S(1)} %max.9), kind=kLoop, calls=%fused_computation.2 | loop fusion | flops 7859200 | bytes 10526720 | tf_op jit(solution)/shard_map/reduce_sum | solution.py:76
  159.1 4.4 %copy.46 = bf16[512,2560]{0,1:T(8,128)(2,1)} copy(bf16[512,2560]{1,0:T(8,128)(2,1)} %all-gather.3.cloned.1.call-done) | data formatting | bytes 5242880 | tf_op jit(solution)/shard_map/all_gather | solution.py:51
  163.5 2.0 broadcast_select_fusion
  165.5 5.3 %fusion.2 = f32[20,256,128]{2,1,0:T(8,128)S(1)} fusion(bf16[512,20,128]{0,2,1:T(8,128)(2,1)S(1)} %bitcast.26, f32[20,256,512]{2,1,0:T(8,128)} %get-tuple-element.8, f32[20,256]{1,0:T(8,128)S(1)} %max.9), kind=kOutput, calls=%fused_computation.4 | convolution fusion | flops 678952960 | bytes 15749120 | tf_op jit(solution)/shard_map/hrk,khd->hrd/dot_general | solution.py:78
  170.9 2.5 add_multiply_fusion
  173.5 3.2 %reduce-scatter.10.cloned.1.call-done = f32[64,20]{1,0:T(8,128)} async-done(((f32[256,20]{1,0:T(8,128)}), f32[64,20]{1,0:T(8,128)}) %reduce-scatter.10.cloned.1.call-update) | async-done | bytes 5136
  176.7 0.8 copy.60
  177.5 51.7 %reduce-scatter.6.cloned.1.call-done = f32[20,64,128]{2,1,0:T(8,128)} async-done(((f32[20,256,128]{2,1,0:T(8,128)}), f32[20,64,128]{2,1,0:T(8,128)}) %reduce-scatter.6.cloned.1.call-update) | async-done | bytes 655376 | tf_op jit(solution)/shard_map/reduce_scatter | solution.py:87
  229.2 2.1 divide_convert_fusion
  231.3 31.9 %all-gather.5.cloned.1.call-done = bf16[20,256,128]{2,1,0:T(8,128)(2,1)} async-done(((bf16[20,64,128]{2,1,0:T(8,128)(2,1)}), bf16[20,256,128]{2,1,0:T(8,128)(2,1)}) %all-gather.5.cloned.1.call-update) | async-done | bytes 1310736 | tf_op jit(solution)/shard_map/all_gather | solution.py:93
  263.2 6.2 %convolution_bitcast_fusion = f32[256,1280]{1,0:T(8,128)} fusion(bf16[20,256,128]{2,1,0:T(8,128)(2,1)} %all-gather.5.cloned.1.call-done, bf16[20,128,1280]{2,1,0:T(8,128)(2,1)} %bitcast.33), kind=kOutput, calls=%fused_computation.9 | convolution fusion | flops 1677721600 | bytes 9175040 | tf_op jit(solution)/shard_map/hrd,hdc->rc/dot_general | solution.py:95
  270.6 21.4 %reduce-scatter.8.cloned.1.call-done = f32[256,640]{1,0:T(8,128)} async-done(((f32[256,1280]{1,0:T(8,128)}), f32[256,640]{1,0:T(8,128)}) %reduce-scatter.8.cloned.1.call-update) | async-done | bytes 655376 | tf_op jit(solution)/shard_map/reduce_scatter | solution.py:98
  292.0 1.9 multiply_convert_fusion
  (42 shorter events, 4.6 us)
Async XLA Ops:
  7.4 262.8 %copy-start = (f32[256,640]{1,0:T(8,128)S(1)}, f32[256,640]{1,0:T(8,128)}, u32[]{:S(2)}) copy-start(f32[256,640]{1,0:T(8,128)} %param.21) | copy-start | bytes 1966084
  7.4 151.7 %all-gather.3.cloned.1.call-start = ((), (), s32[]{:S(2)}) async-start(), calls=%async_computation.3 | async-start | bytes 2949120 | tf_op jit(solution)/shard_map/all_gather | solution.py:51
  7.4 9.4 %collective-permute-start = (bf16[64,2560]{1,0:T(8,128)(2,1)}, bf16[64,2560]{1,0:T(8,128)(2,1)S(1)}, u32[]{:S(2)}, u32[]{:S(2)}) collective-permute-start(bf16[64,2560]{1,0:T(8,128)(2,1)} %param.16), channel_id=1, source_target_pairs={{0,13},{1,0},{4,1},{5,4},{8,5},{9,8},{12,9},{13,12},{2,15},{3,2},{... | collective-permute-start | bytes 983048 | tf_op jit(solution)/shard_map/ppermute | solution.py:17
  13.2 37.5 %copy-start.1 = (bf16[64,2560]{0,1:T(8,128)(2,1)}, bf16[64,2560]{0,1:T(8,128)(2,1)S(1)}, u32[]{:S(2)}) copy-start(bf16[64,2560]{0,1:T(8,128)(2,1)S(1)} %copy.36) | copy-start | bytes 983044
  17.1 33.6 %copy-start.2 = (bf16[64,2560]{0,1:T(8,128)(2,1)}, bf16[64,2560]{0,1:T(8,128)(2,1)S(1)}, u32[]{:S(2)}) copy-start(bf16[64,2560]{0,1:T(8,128)(2,1)S(1)} %copy.37) | copy-start | bytes 983044
  18.4 32.4 %collective-permute-start.1 = (bf16[128,2560]{0,1:T(8,128)(2,1)}, bf16[128,2560]{0,1:T(8,128)(2,1)}, u32[]{:S(2)}, u32[]{:S(2)}) collective-permute-start(bf16[128,2560]{0,1:T(8,128)(2,1)} %pad_maximum_fusion.1), channel_id=1, source_target_pairs={{0,12},{1,13},{4,0},{5,1},{8,4},{9,5},{12,8},{13,9},{2,14},{3,15},... | collective-permute-start | bytes 1966088 | tf_op jit(solution)/shard_map/ppermute | solution.py:17
  19.0 157.7 %reduce-scatter.10.cloned.1.call-start = ((), (), s32[]{:S(2)}) async-start(), calls=%async_computation.7 | async-start | bytes 163840
  45.5 7.1 %copy-start.7 = (f32[2560]{0:T(1024)S(1)}, f32[2560]{0:T(1024)}, u32[]{:S(2)}) copy-start(f32[2560]{0:T(1024)} %param.13) | copy-start | bytes 30724
  50.8 3.4 %copy-start.6 = (bf16[128,2560]{0,1:T(8,128)(2,1)S(1)}, bf16[128,2560]{0,1:T(8,128)(2,1)}, u32[]{:S(2)}) copy-start(bf16[128,2560]{0,1:T(8,128)(2,1)} %copy.43) | copy-start | bytes 1966084
  52.5 59.1 %collective-permute-start.2 = (bf16[256,2560]{0,1:T(8,128)(2,1)S(1)}, bf16[256,2560]{0,1:T(8,128)(2,1)}, u32[]{:S(2)}, u32[]{:S(2)}) collective-permute-start(bf16[256,2560]{0,1:T(8,128)(2,1)S(1)} %pad_maximum_fusion), channel_id=1, source_target_pairs={{0,8},{1,9},{4,12},{5,13},{8,0},{9,1},{12,4},{13,5},{2,10},{3,11},... | collective-permute-start | bytes 3932168 | tf_op jit(solution)/shard_map/ppermute | solution.py:17
  53.0 1.2 copy-start.3
  121.5 4.4 %copy-start.4 = (bf16[256,2560]{0,1:T(8,128)(2,1)S(1)}, bf16[256,2560]{0,1:T(8,128)(2,1)}, u32[]{:S(2)}) copy-start(bf16[256,2560]{0,1:T(8,128)(2,1)} %copy-done.3) | copy-start | bytes 3932164
  158.8 70.4 %reduce-scatter.6.cloned.1.call-start = ((), (), s32[]{:S(2)}) async-start(), calls=%async_computation.4 | async-start | bytes 3276800 | tf_op jit(solution)/shard_map/reduce_scatter | solution.py:87
  165.5 5.4 %copy-start.5 = (bf16[128,2560]{0,1:T(8,128)(2,1)S(1)}, bf16[128,2560]{0,1:T(8,128)(2,1)}, u32[]{:S(2)}) copy-start(bf16[128,2560]{0,1:T(8,128)(2,1)} %copy.49) | copy-start | bytes 1966084
  173.4 89.8 %all-gather.5.cloned.1.call-start = ((), (), s32[]{:S(2)}) async-start(), calls=%async_computation.5 | async-start | bytes 1638400 | tf_op jit(solution)/shard_map/all_gather | solution.py:93
  231.3 60.7 %reduce-scatter.8.cloned.1.call-start = ((), (), s32[]{:S(2)}) async-start(), calls=%async_computation.6 | async-start | bytes 1966080 | tf_op jit(solution)/shard_map/reduce_scatter | solution.py:98
Sparse Core Ops, SparseCore 0:
  19.1 38.6 all-gather.2
  269.5 22.4 reduce-scatter.7
Sparse Core Ops, SparseCore 1:
  158.9 17.7 reduce-scatter.9
  178.8 50.3 reduce-scatter.5
  231.4 31.8 all-gather.4
